TPU v7x, 32 devices: a whole 2x2x4 slice. The times are simulated.
32 devices in a mesh: tm: 16 (over z, y, core), head: 2 (over x).
Axes of the slice: x: 2, y: 2, z: 4, core: 2. Of those that a mesh axis runs over, the one named last changes fastest.
Arguments:
- codes: int32 [16384, 8], P('tm'), may hold values from 0 to 1023
- tables: bfloat16 [8, 1024, 2048], P(None, None, 'head'), may hold values from -2.5 to 2.5
- conv_weight: bfloat16 [5, 2048, 2048], P(None, 'head'), may hold values from -0.0625 to 0.0625
- norm_gain: float32 [2048], replicated, may hold values from 0.1 to 1.9
- key_weight: bfloat16 [2048, 2048], P(None, 'head')
- value_weight: bfloat16 [2048, 2048], P(None, 'head'), may hold values from -0.125 to 0.125
- query_weight: bfloat16 [2048, 2048], P(None, 'head')
- latent_pos: int32 [512], replicated, may hold values from 0 to 4095, as said below
Outputs:
- attended: bfloat16 [512, 2048], P('tm', 'head')
Inputs may be any that keep to these rules, and one draw needn't show every extreme that they name: `latent_pos`: strictly increasing; holds every multiple of 256 and the last row 4095.
All inputs are finite; a program needn't handle non-finite values.
Results may differ from a plain program's by a relative error of at most 0.04.
The roundings to bfloat16 on the way count: a program that leaves them out, or rounds other values in their place, can miss the bound.
Values may be sent and summed in bfloat16 or wider, within the bound.
No kernel may reach another device: no remote copies, remote signals or barrier semaphores. Data moves between devices by JAX's collectives and lax.ppermute only.
A program may use at most 128 MiB of HBM per device.

v0:
```python
import math
import jax
import jax.numpy as jnp
from jax import lax
from jax.sharding import PartitionSpec as P

D = 2048
HEAD_DIM = 128
STRIDE = 4


def passed_along(value, axis, steps):
    count = lax.axis_size(axis)
    leading, last = (max(0, -steps), min(count, count - steps))
    return lax.ppermute(value, axis, [(source, source + steps) for source in range(leading, last)])


def on_device(
    codes, tables, conv_weight, norm_gain, key_weight, value_weight, query_weight, latent_pos
):
    frame_count = codes.shape[0]
    local_width = tables.shape[2]
    summed = jnp.zeros((frame_count, local_width), jnp.float32)
    for codebook in range(codes.shape[1]):
        summed = summed + jnp.take(tables[codebook], codes[:, codebook], axis=0).astype(jnp.float32)
    frames = summed.astype(jnp.bfloat16)
    taps = conv_weight.shape[0]
    lag_rows = taps - STRIDE
    row_count = frame_count // STRIDE
    previous = passed_along(frames[frame_count - lag_rows :], "tm", 1)
    padded = jnp.concatenate([previous, frames], 0)
    earlier = (
        padded[:frame_count]
        .reshape(row_count, STRIDE, local_width)[:, :lag_rows]
        .reshape(row_count, lag_rows * local_width)
    )
    latter = frames.reshape(row_count, STRIDE * local_width)
    window = jnp.concatenate([earlier, latter], 1)
    partial_value = jnp.dot(
        window,
        conv_weight.reshape(taps * local_width, conv_weight.shape[2]),
        preferred_element_type=jnp.float32,
    )
    portion = lax.psum_scatter(partial_value, "head", scatter_dimension=1, tiled=True).astype(
        jnp.bfloat16
    )
    widened = lax.all_gather(portion, "head", axis=1, tiled=True).astype(jnp.float32)
    scaled = (widened * norm_gain[None, :]).astype(jnp.bfloat16)
    key_acc = jnp.dot(scaled, key_weight, preferred_element_type=jnp.float32)
    value_acc = jnp.dot(scaled, value_weight, preferred_element_type=jnp.float32)
    query_acc = jnp.dot(scaled, query_weight, preferred_element_type=jnp.float32)
    squares = jnp.sum(widened * widened, 1)
    inverse = lax.rsqrt(squares / D + 1e-06)
    key_rows = (inverse[:, None] * key_acc).astype(jnp.bfloat16)
    value_rows = (inverse[:, None] * value_acc).astype(jnp.bfloat16)
    query_rows = (inverse[:, None] * query_acc).astype(jnp.bfloat16)
    first_row = lax.axis_index("tm") * row_count
    positions = first_row + jnp.arange(row_count, dtype=jnp.int32)
    selector = (latent_pos[:, None] == positions[None, :]).astype(jnp.bfloat16)
    selected = jnp.dot(selector, query_rows, preferred_element_type=jnp.float32)
    queries = lax.psum(selected.astype(jnp.bfloat16), "tm")
    latent_count = latent_pos.shape[0]
    group_heads = key_weight.shape[1] // HEAD_DIM
    query_three = queries.reshape(latent_count, group_heads, HEAD_DIM)
    key_three = key_rows.reshape(row_count, group_heads, HEAD_DIM)
    value_three = value_rows.reshape(row_count, group_heads, HEAD_DIM)
    scores = jnp.einsum(
        "lhd,rhd->hlr", query_three, key_three, preferred_element_type=jnp.float32
    ) * (1.0 / math.sqrt(HEAD_DIM))
    visible = (positions[None, :] <= latent_pos[:, None])[None, :, :]
    scores = jnp.where(visible, scores, -1e30)
    largest = jnp.max(scores, 2)
    weights = jnp.exp(scores - largest[:, :, None]) * visible.astype(jnp.float32)
    row_sums = jnp.sum(weights, 2)
    product = jnp.einsum(
        "hlr,rhd->lhd",
        weights.astype(jnp.bfloat16),
        value_three,
        preferred_element_type=jnp.float32,
    )
    product = product.reshape(latent_count, group_heads * HEAD_DIM)
    peaks = largest.T
    totals = row_sums.T
    peak_all = lax.pmax(peaks, "tm")
    factor = jnp.exp(peaks - peak_all)
    rescaled = product * jnp.repeat(factor, HEAD_DIM, axis=1)
    output_mine, total_mine = (
        lax.psum_scatter(
            rescaled.astype(jnp.bfloat16), "tm", scatter_dimension=0, tiled=True
        ).astype(jnp.float32),
        lax.psum_scatter(
            (totals * factor).astype(jnp.bfloat16), "tm", scatter_dimension=0, tiled=True
        ).astype(jnp.float32),
    )
    return (output_mine / jnp.repeat(total_mine, HEAD_DIM, axis=1)).astype(jnp.bfloat16)


def solution(mesh):
    placed = (
        P("tm", None),
        P(None, None, "head"),
        P(None, "head", None),
        P(),
        P(None, "head"),
        P(None, "head"),
        P(None, "head"),
        P(),
    )
    return jax.shard_map(
        on_device, mesh=mesh, in_specs=placed, out_specs=P("tm", "head"), check_vma=False
    )
```

profile of v0, /device:TPU:0, one launch (start us, length us, event | category | flops | bytes accessed | tf_op | source)
XLA Modules:
  0.0 457.3 jit_solution(12597088900499182918)
XLA Ops:
  6.5 0.0 reduce-scatter.6.cloned.1.call-start
  6.5 1.1 fusion.50
  7.8 11.5 %slice_bitcast_fusion.7 = (bf16[1024,1024]{1,0:T(8,128)(2,1)}, bf16[1024,1024]{1,0:T(8,128)(2,1)}, bf16[1024,1024]{1,0:T(8,128)(2,1)}, bf16[1024,1024]{1,0:T(8,1...) fusion(bf16[8,1024,1024]{2,1,0:T(8,128)(2,1)} %param.11), kind=kLoop, calls=%fused_computation.37 | loop fusion | bytes 33554432 | tf_op jit(solution)/shard_map/squeeze | solution.py:25
  19.2 7.9 %gather_fusion.2 = bf16[1024,1024]{1,0:T(8,128)(2,1)} fusion(bf16[1024,1024]{1,0:T(8,128)(2,1)} %get-tuple-element.12, s32[1024]{0:T(1024)S(1)} %fusion.40), kind=kCustom, calls=%fused_computation.2.clone | custom fusion | bytes 4198400 | tf_op jit(solution)/shard_map/jit(_take)/gather | solution.py:25
  27.1 7.9 %gather_fusion.3 = bf16[1024,1024]{1,0:T(8,128)(2,1)} fusion(bf16[1024,1024]{1,0:T(8,128)(2,1)} %get-tuple-element.11, s32[1024]{0:T(1024)S(1)} %fusion.41), kind=kCustom, calls=%fused_computation.3.clone | custom fusion | bytes 4198400 | tf_op jit(solution)/shard_map/jit(_take)/gather | solution.py:25
  35.0 7.9 %gather_fusion.4 = bf16[1024,1024]{1,0:T(8,128)(2,1)} fusion(bf16[1024,1024]{1,0:T(8,128)(2,1)} %get-tuple-element.10, s32[1024]{0:T(1024)S(1)} %fusion.42), kind=kCustom, calls=%fused_computation.4.clone | custom fusion | bytes 4198400 | tf_op jit(solution)/shard_map/jit(_take)/gather | solution.py:25
  42.9 7.9 %gather_fusion.5 = bf16[1024,1024]{1,0:T(8,128)(2,1)} fusion(bf16[1024,1024]{1,0:T(8,128)(2,1)} %get-tuple-element.9, s32[1024]{0:T(1024)S(1)} %fusion.43), kind=kCustom, calls=%fused_computation.5.clone | custom fusion | bytes 4198400 | tf_op jit(solution)/shard_map/jit(_take)/gather | solution.py:25
  50.8 7.9 %gather_fusion.6 = bf16[1024,1024]{1,0:T(8,128)(2,1)} fusion(bf16[1024,1024]{1,0:T(8,128)(2,1)} %get-tuple-element.15, s32[1024]{0:T(1024)S(1)} %fusion.44), kind=kCustom, calls=%fused_computation.6.clone | custom fusion | bytes 4198400 | tf_op jit(solution)/shard_map/jit(_take)/gather | solution.py:25
  58.7 7.9 %gather_fusion.7 = bf16[1024,1024]{1,0:T(8,128)(2,1)} fusion(bf16[1024,1024]{1,0:T(8,128)(2,1)} %get-tuple-element.14, s32[1024]{0:T(1024)S(1)} %fusion.45), kind=kCustom, calls=%fused_computation.7.clone | custom fusion | bytes 4198400 | tf_op jit(solution)/shard_map/jit(_take)/gather | solution.py:25
  66.5 7.9 %gather_fusion = bf16[1024,1024]{1,0:T(8,128)(2,1)} fusion(bf16[1024,1024]{1,0:T(8,128)(2,1)} %get-tuple-element.8, s32[1024]{0:T(1024)S(1)} %fusion.38), kind=kCustom, calls=%fused_computation.clone | custom fusion | bytes 4198400 | tf_op jit(solution)/shard_map/jit(_take)/gather | solution.py:25
  74.4 5.3 %gather_fusion.1 = bf16[1024,1024]{1,0:T(8,128)(2,1)} fusion(bf16[1024,1024]{1,0:T(8,128)(2,1)S(1)} %get-tuple-element.13, s32[1024]{0:T(1024)S(1)} %fusion.39), kind=kCustom, calls=%fused_computation.1.clone | custom fusion | bytes 4198400 | tf_op jit(solution)/shard_map/jit(_take)/gather | solution.py:25
  79.8 8.3 %add_convert_fusion = bf16[1024,1024]{1,0:T(8,128)(2,1)S(1)} fusion(bf16[1024,1024]{1,0:T(8,128)(2,1)} %gather_fusion.7, bf16[1024,1024]{1,0:T(8,128)(2,1)} %gather_fusion.6, bf16[1024,1024]{1,0:T(8,128)(2,1)} %gather_fusion.5, bf16[1024,1024]{1,0:T(8,128)(2,1)} %gather_fusion.4, bf16[1024,1024]{1,0:T(8,128)(2,1)} %gather_fusion.3, ...), kind=kLoop, calls=%fused_computation.10 | loop fusion | flops 25165824 | bytes 18882560 | tf_op jit(solution)/shard_map/convert_element_type | solution.py:26
  88.1 2.6 collective-permute-start
  90.6 2.6 reshape.99
  93.2 0.0 collective-permute-done
  93.2 1.9 pad_maximum_fusion
  95.1 2.7 reshape.97
  97.8 0.0 copy-start
  97.8 0.7 slice.93
  98.6 0.2 copy.41
  98.7 0.7 copy-done
  99.4 11.2 %fusion.3 = f32[256,2048]{1,0:T(8,128)} fusion(bf16[5120,2048]{1,0:T(8,128)(2,1)} %bitcast.87, bf16[256,4096]{1,0:T(8,128)(2,1)S(1)} %copy-done, bf16[256,1024]{1,0:T(8,128)(2,1)S(1)} %bitcast.67), kind=kOutput, calls=%fused_computation.16 | convolution fusion | flops 5373952000 | bytes 25690112 | tf_op jit(solution)/shard_map/dot_general | solution.py:39
  110.7 0.0 copy-start.2
  110.7 0.0 reduce-scatter.6.cloned.1.call-update
  110.7 0.0 copy-start.3
  110.7 0.0 all-gather.2.cloned.1.call-start
  110.7 34.5 %reduce-scatter.6.cloned.1.call-done = f32[256,1024]{1,0:T(8,128)} async-done(((f32[256,2048]{1,0:T(8,128)}), f32[256,1024]{1,0:T(8,128)}) %reduce-scatter.6.cloned.1.call-update) | async-done | bytes 1048592 | tf_op jit(solution)/shard_map/reduce_scatter | solution.py:44
  145.3 2.1 convert_element_type.87
  147.4 0.0 all-gather.2.cloned.1.call-update
  147.4 0.0 all-reduce.2.cloned.1.call-start
  147.5 0.0 copy-done.2
  147.5 0.2 broadcast_compare_fusion
  147.7 21.2 %all-gather.2.cloned.1.call-done = bf16[256,2048]{1,0:T(8,128)(2,1)} async-done(((bf16[256,1024]{1,0:T(8,128)(2,1)}), bf16[256,2048]{1,0:T(8,128)(2,1)}) %all-gather.2.cloned.1.call-update) | async-done | bytes 1048592 | tf_op jit(solution)/shard_map/all_gather | solution.py:47
  168.9 1.5 fusion.7
  170.4 0.0 copy-done.3
  170.4 4.0 fusion.19
  174.4 0.0 copy-start.1
  174.5 1.2 copy.40
  175.7 0.0 all-reduce.2.cloned.1.call-update
  175.7 0.0 reduce-scatter.10.cloned.1.call-start
  175.7 0.2 copy-done.1
  175.9 3.4 fusion.20
  179.4 0.2 copy.24
  179.6 3.6 fusion.23
  183.1 86.5 %all-reduce.2.cloned.1.call-done = bf16[512,8,128]{2,0,1:T(8,128)(2,1)} async-done(((bf16[512,8,128]{2,0,1:T(8,128)(2,1)}), bf16[512,8,128]{2,0,1:T(8,128)(2,1)}) %all-reduce.2.cloned.1.call-update) | async-done | bytes 1048592 | tf_op jit(solution)/shard_map/psum | solution.py:61
  269.7 4.0 fusion
  273.7 58.4 %pmax.7 = f32[512,8]{0,1:T(8,128)S(1)} all-reduce(f32[512,8]{0,1:T(8,128)S(1)} %bitcast.70), channel_id=1, replica_groups=mesh['tm'=16,'head'=2] {'tm'}, use_global_device_ids=true, to_apply=%region_4.6 | all-reduce | flops 4096 | bytes 32768 | tf_op jit(solution)/shard_map/pmax | solution.py:84
  332.1 3.2 fusion.1
  335.3 0.8 copy.25
  336.1 0.0 reduce-scatter.10.cloned.1.call-update
  336.1 0.0 reduce-scatter.8.cloned.1.call-start
  336.2 3.6 fusion.11
  339.8 1.3 copy.21
  341.1 0.0 reduce-scatter.8.cloned.1.call-update
  341.1 48.0 %reduce-scatter.10.cloned.1.call-done = bf16[32,8]{1,0:T(8,128)(2,1)} async-done(((bf16[512,8]{1,0:T(8,128)(2,1)}), bf16[32,8]{1,0:T(8,128)(2,1)}) %reduce-scatter.10.cloned.1.call-update) | async-done | bytes 528
  389.2 0.8 copy.26
  389.9 0.1 copy.22
  390.0 59.2 %reduce-scatter.8.cloned.1.call-done = bf16[32,1024]{1,0:T(8,128)(2,1)} async-done(((bf16[512,1024]{1,0:T(8,128)(2,1)}), bf16[32,1024]{1,0:T(8,128)(2,1)}) %reduce-scatter.8.cloned.1.call-update) | async-done | bytes 65552 | tf_op jit(solution)/shard_map/reduce_scatter | solution.py:88
  449.2 0.1 broadcast_in_dim.40
  449.3 1.5 fusion.36
  (16 shorter events, 0.1 us)
Async XLA Ops:
  6.5 138.8 %reduce-scatter.6.cloned.1.call-start = ((), (), s32[]{:S(2)}) async-start(), calls=%async_computation.3 | async-start | bytes 3145728 | tf_op jit(solution)/shard_map/reduce_scatter | solution.py:44
  88.1 5.1 %collective-permute-start = (bf16[1,1024]{1,0:T(2,128)(2,1)S(1)}, bf16[1,1024]{1,0:T(2,128)(2,1)S(1)}, u32[]{:S(2)}, u32[]{:S(2)}) collective-permute-start(bf16[1,1024]{1,0:T(2,128)(2,1)S(1)} %slice.92), channel_id=1, source_target_pairs={{0,2},{2,4},{4,6},{6,8},{8,10},{10,12},{12,14},{14,16},{16,18},{18... | collective-permute-start | bytes 6152 | tf_op jit(solution)/shard_map/ppermute | solution.py:15
  97.8 1.6 copy-start
  110.7 36.8 %copy-start.2 = (s32[512]{0:T(512)S(1)}, s32[512]{0:T(512)}, u32[]{:S(2)}) copy-start(s32[512]{0:T(512)} %param.17) | copy-start | bytes 6148
  110.7 59.7 %copy-start.3 = (f32[2048]{0:T(1024)S(1)}, f32[2048]{0:T(1024)}, u32[]{:S(2)}) copy-start(f32[2048]{0:T(1024)} %param.13) | copy-start | bytes 24580
  110.7 58.2 %all-gather.2.cloned.1.call-start = ((), (), s32[]{:S(2)}) async-start(), calls=%async_computation.4 | async-start | bytes 1572864 | tf_op jit(solution)/shard_map/all_gather | solution.py:47
  147.4 122.3 %all-reduce.2.cloned.1.call-start = ((), (), s32[]{:S(2)}) async-start(), calls=%async_computation.5 | async-start | bytes 2097152 | tf_op jit(solution)/shard_map/psum | solution.py:61
  174.4 1.5 copy-start.1
  175.7 213.5 %reduce-scatter.10.cloned.1.call-start = ((), (), s32[]{:S(2)}) async-start(), calls=%async_computation.7 | async-start | bytes 139264
  336.1 113.1 %reduce-scatter.8.cloned.1.call-start = ((), (), s32[]{:S(2)}) async-start(), calls=%async_computation.6 | async-start | bytes 1114112 | tf_op jit(solution)/shard_map/reduce_scatter | solution.py:88
Sparse Core Ops, SparseCore 0:
  110.8 34.4 reduce-scatter.5
  147.5 21.2 all-gather.1
  175.8 93.8 all-reduce.1
  336.2 52.8 reduce-scatter.9
  392.6 56.5 reduce-scatter.7
where the time goes:
time: 458 us; the launch traced here: 457 us
  waiting for transfers between devices  250 us (55%)
  local copies, waits for them, and re-layouts  84.5 us (18%)
  blocking collectives  58.4 us (13%)
  matrix products  29.9 us (7%)
  other arithmetic  18.7 us (4%)
  between operations  13.4 us (3%)
    psum x1, waiting for transfers between devices, on_device(): queries = lax.psum(selected.astype(jnp.bfloat16), 'tm')  86.5 us
    gather x8, local copies, waits for them, and re-layouts, on_device(): jnp.take(tables[codebook], codes[:, codebook], axis=0).astype(jnp.float32)  60.5 us
    reduce_scatter x1, waiting for transfers between devices, on_device(): lax.psum_scatter(rescaled.astype(jnp.bfloat16), 'tm', scatter_dimension=0...  59.2 us
    pmax x1, blocking collectives, on_device(): peak_all = lax.pmax(peaks, 'tm')  58.4 us
    unnamed x6, waiting for transfers between devices  48.1 us
    reduce_scatter x1, waiting for transfers between devices, on_device(): lax.psum_scatter(partial_value, 'head', scatter_dimension=1, tiled=True)  34.5 us
    all_gather x1, waiting for transfers between devices, on_device(): lax.all_gather(portion, 'head', axis=1, tiled=True).astype(jnp.float32)  21.2 us
    squeeze x1, local copies, waits for them, and re-layouts, on_device(): tables[codebook]  11.5 us
  transfers between devices with their start and end apart: 6, of which 5 were waited for; matrix products, arithmetic and copies ran while one was open for 3% of the time, Pallas kernels for 0%

commit v1 on v0

--- a/solution.py
+++ b/solution.py
@@ -58,7 +58,7 @@
     positions = first_row + jnp.arange(row_count, dtype=jnp.int32)
     selector = (latent_pos[:, None] == positions[None, :]).astype(jnp.bfloat16)
     selected = jnp.dot(selector, query_rows, preferred_element_type=jnp.float32)
-    queries = lax.psum(selected.astype(jnp.bfloat16), "tm")
+    queries = jnp.sum(lax.all_gather(selected.astype(jnp.bfloat16), "tm"), axis=0)
     latent_count = latent_pos.shape[0]
     group_heads = key_weight.shape[1] // HEAD_DIM
     query_three = queries.reshape(latent_count, group_heads, HEAD_DIM)

time: 458 us -> 500 us (1.092)
  waiting for transfers between devices: 250 us -> 282 us
  other arithmetic: 18.7 us -> 28.1 us
    all_gather x0 -> x1, waiting for transfers between devices: none -> 118 us  [on_device(): lax.all_gather(selected.astype(jnp.bfloat16), 'tm')]
    psum x1 -> x0, waiting for transfers between devices: 86.5 us -> none  [on_device(): queries = lax.psum(selected.astype(jnp.bfloat16), 'tm')]
    reduce_sum x0 -> x1, other arithmetic: none -> 9.33 us  [on_device(): jnp.sum(lax.all_gather(selected.astype(jnp.bfloat16), 'tm'), axis=0)]
where the time goes in v1:
time: 500 us; the launch traced here: 499 us
  waiting for transfers between devices  282 us (56%)
  local copies, waits for them, and re-layouts  84.7 us (17%)
  blocking collectives  58.7 us (12%)
  matrix products  29.7 us (6%)
  other arithmetic  28.1 us (6%)
  between operations  13.4 us (3%)
    all_gather x1, waiting for transfers between devices, on_device(): lax.all_gather(selected.astype(jnp.bfloat16), 'tm')  118 us
    gather x8, local copies, waits for them, and re-layouts, on_device(): jnp.take(tables[codebook], codes[:, codebook], axis=0).astype(jnp.float32)  60.7 us
    reduce_scatter x1, waiting for transfers between devices, on_device(): lax.psum_scatter(rescaled.astype(jnp.bfloat16), 'tm', scatter_dimension=0...  59.3 us
    pmax x1, blocking collectives, on_device(): peak_all = lax.pmax(peaks, 'tm')  58.7 us
    unnamed x6, waiting for transfers between devices  48.1 us
    reduce_scatter x1, waiting for transfers between devices, on_device(): lax.psum_scatter(partial_value, 'head', scatter_dimension=1, tiled=True)  34.5 us
    all_gather x1, waiting for transfers between devices, on_device(): lax.all_gather(portion, 'head', axis=1, tiled=True).astype(jnp.float32)  21.4 us
    squeeze x1, local copies, waits for them, and re-layouts, on_device(): tables[codebook]  11.4 us
  transfers between devices with their start and end apart: 6, of which 5 were waited for; matrix products, arithmetic and copies ran while one was open for 3% of the time, Pallas kernels for 0%

profile of v1, /device:TPU:0, one launch (start us, length us, event | category | flops | bytes accessed | tf_op | source)
XLA Modules:
  0.0 499.2 jit_solution(15770851519805647847)
XLA Ops:
  6.5 0.0 reduce-scatter.6.cloned.1.call-start
  6.5 1.1 fusion.48
  7.8 11.4 %slice_bitcast_fusion.7 = (bf16[1024,1024]{1,0:T(8,128)(2,1)}, bf16[1024,1024]{1,0:T(8,128)(2,1)}, bf16[1024,1024]{1,0:T(8,128)(2,1)}, bf16[1024,1024]{1,0:T(8,1...) fusion(bf16[8,1024,1024]{2,1,0:T(8,128)(2,1)} %param.11), kind=kLoop, calls=%fused_computation.37 | loop fusion | bytes 33554432 | tf_op jit(solution)/shard_map/squeeze | solution.py:25
  19.2 7.9 %gather_fusion.2 = bf16[1024,1024]{1,0:T(8,128)(2,1)} fusion(bf16[1024,1024]{1,0:T(8,128)(2,1)} %get-tuple-element.12, s32[1024]{0:T(1024)S(1)} %fusion.38), kind=kCustom, calls=%fused_computation.2.clone | custom fusion | bytes 4198400 | tf_op jit(solution)/shard_map/jit(_take)/gather | solution.py:25
  27.1 7.9 %gather_fusion.3 = bf16[1024,1024]{1,0:T(8,128)(2,1)} fusion(bf16[1024,1024]{1,0:T(8,128)(2,1)} %get-tuple-element.11, s32[1024]{0:T(1024)S(1)} %fusion.39), kind=kCustom, calls=%fused_computation.3.clone | custom fusion | bytes 4198400 | tf_op jit(solution)/shard_map/jit(_take)/gather | solution.py:25
  35.0 7.9 %gather_fusion.4 = bf16[1024,1024]{1,0:T(8,128)(2,1)} fusion(bf16[1024,1024]{1,0:T(8,128)(2,1)} %get-tuple-element.10, s32[1024]{0:T(1024)S(1)} %fusion.40), kind=kCustom, calls=%fused_computation.4.clone | custom fusion | bytes 4198400 | tf_op jit(solution)/shard_map/jit(_take)/gather | solution.py:25
  42.9 7.9 %gather_fusion.5 = bf16[1024,1024]{1,0:T(8,128)(2,1)} fusion(bf16[1024,1024]{1,0:T(8,128)(2,1)} %get-tuple-element.9, s32[1024]{0:T(1024)S(1)} %fusion.41), kind=kCustom, calls=%fused_computation.5.clone | custom fusion | bytes 4198400 | tf_op jit(solution)/shard_map/jit(_take)/gather | solution.py:25
  50.8 7.9 %gather_fusion.6 = bf16[1024,1024]{1,0:T(8,128)(2,1)} fusion(bf16[1024,1024]{1,0:T(8,128)(2,1)} %get-tuple-element.15, s32[1024]{0:T(1024)S(1)} %fusion.42), kind=kCustom, calls=%fused_computation.6.clone | custom fusion | bytes 4198400 | tf_op jit(solution)/shard_map/jit(_take)/gather | solution.py:25
  58.7 7.9 %gather_fusion.7 = bf16[1024,1024]{1,0:T(8,128)(2,1)} fusion(bf16[1024,1024]{1,0:T(8,128)(2,1)} %get-tuple-element.14, s32[1024]{0:T(1024)S(1)} %fusion.43), kind=kCustom, calls=%fused_computation.7.clone | custom fusion | bytes 4198400 | tf_op jit(solution)/shard_map/jit(_take)/gather | solution.py:25
  66.6 7.9 %gather_fusion = bf16[1024,1024]{1,0:T(8,128)(2,1)} fusion(bf16[1024,1024]{1,0:T(8,128)(2,1)} %get-tuple-element.8, s32[1024]{0:T(1024)S(1)} %fusion.36), kind=kCustom, calls=%fused_computation.clone | custom fusion | bytes 4198400 | tf_op jit(solution)/shard_map/jit(_take)/gather | solution.py:25
  74.6 5.3 %gather_fusion.1 = bf16[1024,1024]{1,0:T(8,128)(2,1)} fusion(bf16[1024,1024]{1,0:T(8,128)(2,1)S(1)} %get-tuple-element.13, s32[1024]{0:T(1024)S(1)} %fusion.37), kind=kCustom, calls=%fused_computation.1.clone | custom fusion | bytes 4198400 | tf_op jit(solution)/shard_map/jit(_take)/gather | solution.py:25
  79.9 8.3 %add_convert_fusion = bf16[1024,1024]{1,0:T(8,128)(2,1)S(1)} fusion(bf16[1024,1024]{1,0:T(8,128)(2,1)} %gather_fusion.7, bf16[1024,1024]{1,0:T(8,128)(2,1)} %gather_fusion.6, bf16[1024,1024]{1,0:T(8,128)(2,1)} %gather_fusion.5, bf16[1024,1024]{1,0:T(8,128)(2,1)} %gather_fusion.4, bf16[1024,1024]{1,0:T(8,128)(2,1)} %gather_fusion.3, ...), kind=kLoop, calls=%fused_computation.10 | loop fusion | flops 25165824 | bytes 18882560 | tf_op jit(solution)/shard_map/convert_element_type | solution.py:26
  88.2 2.6 collective-permute-start
  90.8 2.6 reshape.99
  93.3 0.0 collective-permute-done
  93.4 1.9 pad_maximum_fusion
  95.2 2.7 reshape.97
  98.0 0.0 copy-start
  98.0 0.7 slice.93
  98.7 0.2 copy.46
  98.9 0.7 copy-done
  99.6 11.3 %fusion.3 = f32[256,2048]{1,0:T(8,128)} fusion(bf16[5120,2048]{1,0:T(8,128)(2,1)} %bitcast.85, bf16[256,4096]{1,0:T(8,128)(2,1)S(1)} %copy-done, bf16[256,1024]{1,0:T(8,128)(2,1)S(1)} %bitcast.65), kind=kOutput, calls=%fused_computation.16 | convolution fusion | flops 5373952000 | bytes 25690112 | tf_op jit(solution)/shard_map/dot_general | solution.py:39
  110.8 0.0 reduce-scatter.6.cloned.1.call-update
  110.9 0.0 copy-start.3
  110.9 0.0 copy-start.4
  110.9 0.0 all-gather.4.cloned.1.call-start
  110.9 34.5 %reduce-scatter.6.cloned.1.call-done = f32[256,1024]{1,0:T(8,128)} async-done(((f32[256,2048]{1,0:T(8,128)}), f32[256,1024]{1,0:T(8,128)}) %reduce-scatter.6.cloned.1.call-update) | async-done | bytes 1048592 | tf_op jit(solution)/shard_map/reduce_scatter | solution.py:44
  145.5 2.1 convert_element_type.89
  147.6 0.0 all-gather.4.cloned.1.call-update
  147.6 0.0 all-gather.6.cloned.1.call-start
  147.7 21.4 %all-gather.4.cloned.1.call-done = bf16[256,2048]{1,0:T(8,128)(2,1)} async-done(((bf16[256,1024]{1,0:T(8,128)(2,1)}), bf16[256,2048]{1,0:T(8,128)(2,1)}) %all-gather.4.cloned.1.call-update) | async-done | bytes 1048592 | tf_op jit(solution)/shard_map/all_gather | solution.py:47
  169.0 1.5 fusion.7
  170.6 0.0 copy-done.3
  170.6 0.0 copy-done.4
  170.6 0.0 copy-start.1
  170.6 5.2 %convolution_convert_fusion = bf16[512,1024]{1,0:T(8,128)(2,1)} fusion(bf16[2048,1024]{1,0:T(8,128)(2,1)} %param.16, bf16[256,2048]{1,0:T(8,128)(2,1)} %all-gather.4.cloned.1.call-done, f32[2048]{0:T(1024)S(1)} %copy-done.4, f32[256]{0:T(256)S(1)} %add_rsqrt_fusion, s32[512]{0:T(512)S(1)} %copy-done.3, s32[256]{0:T(256)S(1)} %iota_add_fusion), kind=kOutput, calls=%fused_computation.39 | convolution fusion | flops 1344929792 | bytes 6303744 | tf_op jit(solution)/shard_map/dot_general | solution.py:60
  175.8 0.0 all-gather.6.cloned.1.call-update
  175.8 0.0 reduce-scatter.10.cloned.1.call-start
  175.8 0.2 broadcast_compare_fusion
  176.0 0.0 copy-done.1
  176.0 3.4 fusion.19
  179.4 1.0 copy.32
  180.5 3.4 fusion.22
  183.9 118.5 %all-gather.6.cloned.1.call-done = bf16[8192,1024]{1,0:T(8,128)(2,1)} async-done(((bf16[512,1024]{1,0:T(8,128)(2,1)}), bf16[8192,1024]{1,0:T(8,128)(2,1)}) %all-gather.6.cloned.1.call-update) | async-done | bytes 16777232 | tf_op jit(solution)/shard_map/all_gather | solution.py:61
  302.4 9.3 %reduce_sum.31 = bf16[512,1024]{1,0:T(8,128)(2,1)S(1)} reduce(bf16[16,512,1024]{2,1,0:T(8,128)(2,1)} %bitcast.62, bf16[]{:T(256)} %constant.14.clone.1), dimensions={0}, to_apply=%region_2.4 | reduce | flops 7864320 | bytes 17825794 | tf_op jit(solution)/shard_map/reduce_sum | solution.py:61
  311.7 0.5 copy.23
  312.2 2.8 fusion
  315.1 58.7 %pmax.7 = f32[512,8]{0,1:T(8,128)S(1)} all-reduce(f32[512,8]{0,1:T(8,128)S(1)} %bitcast.68), channel_id=1, replica_groups=mesh['tm'=16,'head'=2] {'tm'}, use_global_device_ids=true, to_apply=%region_4.6 | all-reduce | flops 4096 | bytes 32768 | tf_op jit(solution)/shard_map/pmax | solution.py:84
  373.8 0.0 copy-start.2
  373.8 3.3 fusion.1
  377.0 0.8 copy.33
  377.8 0.0 reduce-scatter.10.cloned.1.call-update
  377.9 0.0 reduce-scatter.8.cloned.1.call-start
  377.9 0.0 copy-done.2
  377.9 3.6 fusion.11
  381.5 1.3 copy.28
  382.8 0.0 reduce-scatter.8.cloned.1.call-update
  382.9 48.0 %reduce-scatter.10.cloned.1.call-done = bf16[32,8]{1,0:T(8,128)(2,1)} async-done(((bf16[512,8]{1,0:T(8,128)(2,1)}), bf16[32,8]{1,0:T(8,128)(2,1)}) %reduce-scatter.10.cloned.1.call-update) | async-done | bytes 528
  430.9 0.8 copy.34
  431.7 0.1 copy.29
  431.8 59.3 %reduce-scatter.8.cloned.1.call-done = bf16[32,1024]{1,0:T(8,128)(2,1)} async-done(((bf16[512,1024]{1,0:T(8,128)(2,1)}), bf16[32,1024]{1,0:T(8,128)(2,1)}) %reduce-scatter.8.cloned.1.call-update) | async-done | bytes 65552 | tf_op jit(solution)/shard_map/reduce_scatter | solution.py:88
  491.1 0.1 broadcast_in_dim.40
  491.2 1.5 fusion.34
  (16 shorter events, 0.1 us)
Async XLA Ops:
  6.5 138.9 %reduce-scatter.6.cloned.1.call-start = ((), (), s32[]{:S(2)}) async-start(), calls=%async_computation.3 | async-start | bytes 3145728 | tf_op jit(solution)/shard_map/reduce_scatter | solution.py:44
  88.2 5.2 %collective-permute-start = (bf16[1,1024]{1,0:T(2,128)(2,1)S(1)}, bf16[1,1024]{1,0:T(2,128)(2,1)S(1)}, u32[]{:S(2)}, u32[]{:S(2)}) collective-permute-start(bf16[1,1024]{1,0:T(2,128)(2,1)S(1)} %slice.92), channel_id=1, source_target_pairs={{0,2},{2,4},{4,6},{6,8},{8,10},{10,12},{12,14},{14,16},{16,18},{18... | collective-permute-start | bytes 6152 | tf_op jit(solution)/shard_map/ppermute | solution.py:15
  98.0 1.6 copy-start
  110.9 59.7 %copy-start.3 = (s32[512]{0:T(512)S(1)}, s32[512]{0:T(512)}, u32[]{:S(2)}) copy-start(s32[512]{0:T(512)} %param.17) | copy-start | bytes 6148
  110.9 59.7 %copy-start.4 = (f32[2048]{0:T(1024)S(1)}, f32[2048]{0:T(1024)}, u32[]{:S(2)}) copy-start(f32[2048]{0:T(1024)} %param.13) | copy-start | bytes 24580
  110.9 58.2 %all-gather.4.cloned.1.call-start = ((), (), s32[]{:S(2)}) async-start(), calls=%async_computation.4 | async-start | bytes 1572864 | tf_op jit(solution)/shard_map/all_gather | solution.py:47
  147.6 154.8 %all-gather.6.cloned.1.call-start = ((), (), s32[]{:S(2)}) async-start(), calls=%async_computation.6 | async-start | bytes 17825792 | tf_op jit(solution)/shard_map/all_gather | solution.py:61
  170.6 5.4 %copy-start.1 = (bf16[256,2048]{1,0:T(8,128)(2,1)S(1)}, bf16[256,2048]{1,0:T(8,128)(2,1)}, u32[]{:S(2)}) copy-start(bf16[256,2048]{1,0:T(8,128)(2,1)} %all-gather.4.cloned.1.call-done) | copy-start | bytes 3145732
  175.8 255.1 %reduce-scatter.10.cloned.1.call-start = ((), (), s32[]{:S(2)}) async-start(), calls=%async_computation.7 | async-start | bytes 139264
  373.8 4.1 copy-start.2
  377.9 113.2 %reduce-scatter.8.cloned.1.call-start = ((), (), s32[]{:S(2)}) async-start(), calls=%async_computation.5 | async-start | bytes 1114112 | tf_op jit(solution)/shard_map/reduce_scatter | solution.py:88
Sparse Core Ops, SparseCore 0:
  111.0 34.4 reduce-scatter.5
  147.7 21.2 all-gather.3
  175.9 126.4 all-gather.5
  378.0 52.8 reduce-scatter.9
  434.4 56.6 reduce-scatter.7
